TPU v7x, 32 devices: a whole 2x2x4 slice. The times are simulated.
32 devices in a mesh: groups: 2 (over x), req: 16 (over z, y, core).
Axes of the slice: x: 2, y: 2, z: 4, core: 2. Of those that a mesh axis runs over, the one named last changes fastest.
Arguments:
- queries: bfloat16 [64, 128, 192], P('groups', 'req'), parts along dimension 0, may hold values from -48 to 48
- absorb_key: bfloat16 [128, 128, 512], P('req'), may hold values from -0.5 to 0.5
- absorb_value: bfloat16 [128, 512, 128], P('req'), may hold values from -0.75 to 0.75
- out_weight: bfloat16 [16384, 5120], P('req'), may hold values from -0.046875 to 0.046875
- latent_cache: bfloat16 [64, 4096, 576], P(('groups', 'req')), parts along dimension 0, may hold values from -12 to 12
- lengths: int32 [64], P(('groups', 'req')), parts along dimension 0, may hold values from 2 to 4096, as said below
- slot_request: int32 [64], P('groups'), parts along dimension 0, may hold values from 0 to 31, each once
Outputs:
- attended: bfloat16 [64, 5120], P(('groups', 'req')), parts along dimension 0
There are 2 independent parts, one for each index of `groups`. A program takes and returns all parts, laid end to end along the dimension named above; an argument that names none is the same for every part. Nothing has to cross between parts.
Inputs may be any that keep to these rules, and one draw needn't show every extreme that they name: Slot j's valid positions are its first lengths[j] ones; some slot of each group holds exactly 4096. `slot_request`: each request stands in exactly one slot.
All inputs are finite; a program needn't handle non-finite values.
Results may differ from a plain program's by a relative error of at most 0.0079.
Values may be sent and summed in bfloat16 or wider, within the bound.
A program may use at most 64 MiB of HBM per device.

v0:
```python
import math

import jax
import jax.numpy as jnp
from jax import lax
from jax.sharding import PartitionSpec as P


def normalize(scores, lengths):
    visible = lax.broadcasted_iota(jnp.int32, (1, 1, scores.shape[2]), 2) < lengths[:, None, None]
    scores = jnp.where(visible, scores, -jnp.inf)
    highest = jnp.max(scores, axis=2, keepdims=True)
    weights = jnp.exp(scores - highest)
    return (weights / jnp.sum(weights, axis=2, keepdims=True)).astype(jnp.bfloat16)


def on_device(queries, absorb_key, absorb_value, out_weight, latent_cache, lengths, slot_request):
    rotary_start = absorb_key.shape[1]
    latent_width = absorb_key.shape[2]
    factor = 1.0 / math.sqrt(queries.shape[2])
    ordered = jnp.take(queries, slot_request, axis=0)
    lifted = jnp.einsum(
        "jhn,hnc->jhc", ordered[:, :, :rotary_start], absorb_key, preferred_element_type=jnp.float32
    )
    absorbed = jnp.concatenate(
        [lifted, ordered[:, :, rotary_start:].astype(jnp.float32)], axis=2
    ).astype(jnp.bfloat16)
    arrived = lax.all_to_all(absorbed, "req", split_axis=0, concat_axis=1, tiled=True)
    scores = (
        jnp.einsum("jhk,jtk->jht", arrived, latent_cache, preferred_element_type=jnp.float32)
        * factor
    )
    probs = normalize(scores, lengths)
    latent = jnp.einsum(
        "jht,jtc->jhc", probs, latent_cache[:, :, :latent_width], preferred_element_type=jnp.float32
    ).astype(jnp.bfloat16)
    returned = lax.all_to_all(latent, "req", split_axis=1, concat_axis=0, tiled=True)
    values = jnp.einsum(
        "jhc,hcv->jhv", returned, absorb_value, preferred_element_type=jnp.float32
    ).astype(jnp.bfloat16)
    flattened = values.reshape(values.shape[0], values.shape[1] * values.shape[2])
    partial_value = jnp.dot(flattened, out_weight, preferred_element_type=jnp.float32)
    summed = lax.psum_scatter(partial_value, "req", scatter_dimension=0, tiled=True)
    return summed.astype(jnp.bfloat16)


def solution(mesh):
    return jax.shard_map(
        on_device,
        mesh=mesh,
        in_specs=(
            P("groups", "req", None),
            P("req", None, None),
            P("req", None, None),
            P("req", None),
            P(("groups", "req"), None, None),
            P(("groups", "req")),
            P("groups"),
        ),
        out_specs=P(("groups", "req"), None),
        check_vma=False,
    )
```

profile of v0, /device:TPU:0, one launch (start us, length us, event | category | flops | bytes accessed | tf_op | source)
XLA Modules:
  0.0 127.3 jit_solution(3734823095178670835)
XLA Ops:
  0.0 0.0 copy-start
  0.0 0.7 compare_select_fusion
  0.8 0.7 compare_and_fusion
  1.4 1.5 %gather_fusion = bf16[32,8,192]{2,1,0:T(8,128)(2,1)S(1)} fusion(bf16[32,8,192]{2,1,0:T(8,128)(2,1)} %param.7, s32[1024]{0:T(1024)S(1)} %pad_clamp_fusion), kind=kCustom, calls=%fused_computation | custom fusion | bytes 196736 | tf_op jit(solution)/shard_map/jit(_take)/gather | solution.py:21
  2.9 0.1 copy_select_fusion
  3.0 0.0 copy-done
  3.0 0.3 fusion.10
  3.3 0.8 copy.18
  4.2 7.4 %all-to-all-start = ((bf16[32,8,576]{2,1,0:T(8,128)(2,1)}), bf16[32,8,576]{2,1,0:T(8,128)(2,1)S(1)}, u32[]{:S(2)}, u32[]{:S(2)}) async-start(bf16[32,8,576]{2,1,0:T(8,128)(2,1)} %copy.18), calls=%async_computation | async-start | bytes 655360 | tf_op jit(solution)/shard_map/all_to_all | solution.py:28
  11.6 0.7 iota_compare_fusion
  12.3 10.3 %all-to-all-done = bf16[32,8,576]{2,1,0:T(8,128)(2,1)S(1)} async-done(((bf16[32,8,576]{2,1,0:T(8,128)(2,1)}), bf16[32,8,576]{2,1,0:T(8,128)(2,1)S(1)}, u32[]{:S(2)}, u32[]{:S(2)}) %all-to-all-start) | async-done | bytes 294944 | tf_op jit(solution)/shard_map/all_to_all | solution.py:28
  22.6 5.6 %fusion.5 = f32[2,128,4096]{2,1,0:T(8,128)S(1)} fusion(bf16[2,4096,576]{1,2,0:T(8,128)(2,1)} %param.11, pred[2,4096]{1,0:T(4,128)(4,1)S(1)} %iota_compare_fusion, bf16[16,2,8,576]{3,2,1,0:T(8,128)(2,1)S(1)} %bitcast.28), kind=kOutput, calls=%fused_computation.7 | convolution fusion | flops 1210056704 | bytes 13934592 | tf_op jit(solution)/shard_map/jhk,jtk->jht/dot_general | solution.py:30
  28.3 0.0 copy-start.1
  28.3 1.9 %copy-done.1 = f32[2,128,4096]{2,1,0:T(8,128)} copy-done((f32[2,128,4096]{2,1,0:T(8,128)}, f32[2,128,4096]{2,1,0:T(8,128)S(1)}, u32[]{:S(2)}) %copy-start.1) | copy-done | bytes 4194328
  30.2 0.8 fusion.19
  31.0 0.0 copy-start.3
  31.0 0.0 copy-start.2
  31.0 8.9 %fusion.7 = bf16[2,128,512]{2,1,0:T(8,128)(2,1)S(1)} fusion(bf16[2,4096,576]{1,2,0:T(8,128)(2,1)} %param.11, f32[2,128]{1,0:T(2,128)S(1)} %fusion.19, f32[2,128,4096]{2,1,0:T(8,128)} %copy-done.1), kind=kOutput, calls=%fused_computation.10 | convolution fusion | flops 1077022976 | bytes 17040384 | tf_op jit(solution)/shard_map/jht,jtc->jhc/dot_general | solution.py:34
  40.0 1.0 copy.22
  40.9 3.5 %all-to-all-start.1 = ((bf16[2,128,512]{2,0,1:T(2,128)(2,1)}), bf16[2,128,512]{2,0,1:T(2,128)(2,1)S(1)}, u32[]{:S(2)}, u32[]{:S(2)}) async-start(bf16[2,128,512]{2,0,1:T(2,128)(2,1)} %copy.22), calls=%async_computation.1 | async-start | bytes 524288 | tf_op jit(solution)/shard_map/all_to_all | solution.py:37
  44.5 0.0 copy-done.3
  44.5 0.6 dynamic-slice
  45.7 8.7 %all-to-all-done.1 = bf16[2,128,512]{2,0,1:T(2,128)(2,1)S(1)} async-done(((bf16[2,128,512]{2,0,1:T(2,128)(2,1)}), bf16[2,128,512]{2,0,1:T(2,128)(2,1)S(1)}, u32[]{:S(2)}, u32[]{:S(2)}) %all-to-all-start.1) | async-done | bytes 262176 | tf_op jit(solution)/shard_map/all_to_all | solution.py:37
  54.5 0.2 copy.38
  54.6 0.1 all_to_all.33
  54.8 0.0 copy-done.2
  54.8 0.3 fusion.11
  55.0 5.9 %fusion.14 = f32[32,5120]{1,0:T(8,128)S(1)} fusion(bf16[1024,5120]{1,0:T(8,128)(2,1)} %param.10, bf16[8,4,8,128]{3,2,1,0:T(8,128)(2,1)S(1)} %fusion.11), kind=kOutput, calls=%fused_computation.20 | convolution fusion | flops 335544320 | bytes 11206656 | tf_op jit(solution)/shard_map/dot_general | solution.py:42
  61.0 65.7 %all-reduce.2 = bf16[32,5120]{1,0:T(8,128)(2,1)S(1)} all-reduce(f32[32,5120]{1,0:T(8,128)S(1)} %fusion.14), channel_id=2, replica_groups=mesh['groups'=2,'req'=16] {'req'}, use_global_device_ids=true, to_apply=%region_2.3.clone | all-reduce | flops 163840 | bytes 983040
  126.6 0.6 dynamic-slice_convert_fusion
  (3 shorter events, 0.1 us)
Async XLA Ops:
  0.0 3.0 %copy-start = (bf16[8,128,512]{2,1,0:T(8,128)(2,1)S(1)}, bf16[8,128,512]{2,1,0:T(8,128)(2,1)}, u32[]{:S(2)}) copy-start(bf16[8,128,512]{2,1,0:T(8,128)(2,1)} %param.8) | copy-start | bytes 3145732
  4.2 18.5 %all-to-all-start = ((bf16[32,8,576]{2,1,0:T(8,128)(2,1)}), bf16[32,8,576]{2,1,0:T(8,128)(2,1)S(1)}, u32[]{:S(2)}, u32[]{:S(2)}) async-start(bf16[32,8,576]{2,1,0:T(8,128)(2,1)} %copy.18), calls=%async_computation | async-start | bytes 655360 | tf_op jit(solution)/shard_map/all_to_all | solution.py:28
  28.3 1.9 %copy-start.1 = (f32[2,128,4096]{2,1,0:T(8,128)}, f32[2,128,4096]{2,1,0:T(8,128)S(1)}, u32[]{:S(2)}) copy-start(f32[2,128,4096]{2,1,0:T(8,128)S(1)} %fusion.5) | copy-start | bytes 12582916
  31.0 13.5 %copy-start.3 = (u32[32]{0:T(128)S(1)}, u32[32]{0:T(128)}, u32[]{:S(2)}) copy-start(u32[32]{0:T(128)} %constant.29) | copy-start | bytes 388
  31.0 23.7 %copy-start.2 = (bf16[8,512,128]{2,1,0:T(8,128)(2,1)S(1)}, bf16[8,512,128]{2,1,0:T(8,128)(2,1)}, u32[]{:S(2)}) copy-start(bf16[8,512,128]{2,1,0:T(8,128)(2,1)} %param.9) | copy-start | bytes 3145732
  40.9 13.5 %all-to-all-start.1 = ((bf16[2,128,512]{2,0,1:T(2,128)(2,1)}), bf16[2,128,512]{2,0,1:T(2,128)(2,1)S(1)}, u32[]{:S(2)}, u32[]{:S(2)}) async-start(bf16[2,128,512]{2,0,1:T(2,128)(2,1)} %copy.22), calls=%async_computation.1 | async-start | bytes 524288 | tf_op jit(solution)/shard_map/all_to_all | solution.py:37
where the time goes:
time: 128 us; the launch traced here: 127 us
  blocking collectives  65.7 us (51%)
  matrix products  21 us (16%)
  waiting for transfers between devices  19 us (15%)
  starting transfers between devices  10.9 us (9%)
  local copies, waits for them, and re-layouts  6.71 us (5%)
  other arithmetic  3.09 us (2%)
    unnamed x1, blocking collectives  65.7 us
    all_to_all x1, waiting for transfers between devices, on_device(): lax.all_to_all(absorbed, 'req', split_axis=0, concat_axis=1, tiled=True)  10.3 us
    dot_general x1, matrix products, on_device(): jnp.einsum('jht,jtc->jhc', probs, latent_cache[:, :, :latent_width], pref...  8.92 us
    all_to_all x1, waiting for transfers between devices, on_device(): lax.all_to_all(latent, 'req', split_axis=1, concat_axis=0, tiled=True)  8.73 us
    all_to_all x1, starting transfers between devices, on_device(): lax.all_to_all(absorbed, 'req', split_axis=0, concat_axis=1, tiled=True)  7.41 us
    dot_general x1, matrix products, on_device(): jnp.dot(flattened, out_weight, preferred_element_type=jnp.float32)  5.92 us
    dot_general x1, matrix products, on_device(): jnp.einsum('jhk,jtk->jht', arrived, latent_cache, preferred_element_type=...  5.64 us
    all_to_all x1, starting transfers between devices, on_device(): lax.all_to_all(latent, 'req', split_axis=1, concat_axis=0, tiled=True)  3.53 us
  transfers between devices with their start and end apart: 2, of which 2 were waited for; matrix products, arithmetic and copies ran while one was open for 1% of the time, Pallas kernels for 0%

commit v1 on v0

v1 whole, which is shorter than its diff:
```python
import functools
import math

import jax
import jax.numpy as jnp
from jax import lax
from jax.experimental import pallas as pl
from jax.experimental.pallas import tpu as pltpu
from jax.sharding import PartitionSpec as P

MESH = pl.DeviceIdType.MESH
LANES = 128
SCORE_TILE = 1024
OUT_TILES = 5


def kernel(
    n, request_ref, length_ref, query_ref, key_hbm, value_hbm, weight_hbm, cache_hbm,
    out_ref,
    key, value, weight, cache, query_rows, rotary_rows, absorbed_rows, absorbed_out, absorbed_in,
    slot_rows, scores, latent_rows, latent_out, latent_in, returned_rows, values,
    partial, partial_out, partial_in,
    load_sem, send_a, recv_a, send_b, recv_b, send_c, recv_c,
):
    requests, heads, width = query_ref.shape
    nope, latent = key_hbm.shape[1:]
    vdim = value_hbm.shape[2]
    slots, _, context = cache_hbm.shape
    tiles = partial_out.shape[0]
    tile = partial_out.shape[3]
    lanes = latent // LANES
    me = lax.axis_index("req")

    barrier = pltpu.get_barrier_semaphore()

    def greet(k, carry):
        pl.semaphore_signal(
            barrier, inc=1, device_id={"req": lax.rem(me + k, n)}, device_id_type=MESH
        )
        return carry

    lax.fori_loop(1, n, greet, 0)

    load_key = pltpu.make_async_copy(key_hbm, key, load_sem.at[0])
    load_value = pltpu.make_async_copy(value_hbm, value, load_sem.at[1])
    load_weight = pltpu.make_async_copy(weight_hbm, weight, load_sem.at[2])
    load_cache = [
        pltpu.make_async_copy(cache_hbm.at[s], cache.at[s], load_sem.at[3 + s])
        for s in range(slots)
    ]
    load_key.start()
    load_cache[0].start()

    for j in range(requests):
        row = query_ref[request_ref[j]].astype(jnp.float32)
        query_rows[j * heads : (j + 1) * heads, :] = row[:, :nope]
        rotary_rows[j * heads : (j + 1) * heads, :] = row[:, nope:]
    load_key.wait()
    for s in range(1, slots):
        load_cache[s].start()
    load_value.start()
    load_weight.start()
    for h in range(heads):
        picked = query_rows[pl.ds(h, requests, stride=heads), :].astype(jnp.bfloat16)
        lifted = jnp.dot(picked, key[h], preferred_element_type=jnp.float32)
        for l in range(lanes):
            absorbed_rows[l, pl.ds(h, requests, stride=heads), :] = lifted[
                :, l * LANES : (l + 1) * LANES
            ]

    def exchange(out, into, send_sem, recv_sem, at):
        def copy(to, source):
            return pltpu.make_async_remote_copy(
                src_ref=out.at[at, to],
                dst_ref=into.at[at, source],
                send_sem=send_sem.at[at, to],
                recv_sem=recv_sem.at[at, source],
                device_id={"req": to},
                device_id_type=MESH,
            )

        def start(k, carry):
            copy(lax.rem(me + k, n), me).start()
            return carry

        def arrive(k, carry):
            other = lax.rem(me + n - k, n)
            copy(other, other).wait_recv()
            return carry

        def leave(k, carry):
            copy(lax.rem(me + k, n), me).wait_send()
            return carry

        return (
            lambda: lax.fori_loop(1, n, start, 0),
            lambda: lax.fori_loop(1, n, arrive, 0),
            lambda: lax.fori_loop(1, n, leave, 0),
        )

    queries_of = [exchange(absorbed_out, absorbed_in, send_a, recv_a, s) for s in range(slots)]
    latents_of = [exchange(latent_out, latent_in, send_b, recv_b, s) for s in range(slots)]
    partials_of = [exchange(partial_out, partial_in, send_c, recv_c, c) for c in range(tiles)]

    for s in range(slots):
        for d in range(n):
            row = (d * slots + s) * heads
            for l in range(lanes):
                absorbed_out[s, d, :, l * LANES : (l + 1) * LANES] = absorbed_rows[
                    l, row : row + heads, :
                ].astype(jnp.bfloat16)
            absorbed_out[s, d, :, latent:] = rotary_rows[row : row + heads, :].astype(jnp.bfloat16)
        if s == 0:
            pl.semaphore_wait(barrier, n - 1)
        queries_of[s][0]()
        absorbed_in[s, me] = absorbed_out[s, me]

    scale = math.log2(math.e) / math.sqrt(width)
    for s in range(slots):
        queries_of[s][1]()
        for i in range(n):
            slot_rows[i * heads : (i + 1) * heads, :] = absorbed_in[s, i].astype(jnp.float32)
        query = slot_rows[...].astype(jnp.bfloat16)
        load_cache[s].wait()
        length = length_ref[s]
        highest = None
        for t in range(0, context, SCORE_TILE):
            score = jnp.dot(
                query, cache[s, :, t : t + SCORE_TILE], preferred_element_type=jnp.float32
            )
            position = t + lax.broadcasted_iota(jnp.int32, (1, SCORE_TILE), 1)
            score = jnp.where(position < length, score, -jnp.inf)
            scores[:, t : t + SCORE_TILE] = score
            top = jnp.max(score, axis=1, keepdims=True)
            highest = top if highest is None else jnp.maximum(highest, top)
        total, mixed = None, None
        for t in range(0, context, SCORE_TILE):
            prob = jnp.exp2((scores[:, t : t + SCORE_TILE] - highest) * scale)
            part = jnp.sum(prob, axis=1, keepdims=True)
            product = lax.dot_general(
                prob.astype(jnp.bfloat16),
                cache[s, :latent, t : t + SCORE_TILE],
                (((1,), (1,)), ((), ())),
                preferred_element_type=jnp.float32,
            )
            total = part if total is None else total + part
            mixed = product if mixed is None else mixed + product
        latent_rows[...] = mixed / total
        for i in range(n):
            latent_out[s, i] = latent_rows[i * heads : (i + 1) * heads, :].astype(jnp.bfloat16)
        latents_of[s][0]()
        latent_in[s, me] = latent_out[s, me]

    load_value.wait()
    for s in range(slots):
        latents_of[s][1]()
        for d in range(n):
            row = (d * slots + s) * heads
            for l in range(lanes):
                returned_rows[l, row : row + heads, :] = latent_in[
                    s, d, :, l * LANES : (l + 1) * LANES
                ].astype(jnp.float32)
    for h in range(heads):
        picked = jnp.concatenate(
            [returned_rows[l, pl.ds(h, requests, stride=heads), :] for l in range(lanes)], axis=1
        ).astype(jnp.bfloat16)
        values[:, h * vdim : (h + 1) * vdim] = jnp.dot(
            picked, value[h], preferred_element_type=jnp.float32
        ).astype(jnp.bfloat16)

    load_weight.wait()
    for c in range(tiles):
        partial[...] = jnp.dot(
            values[...], weight[:, c * tile : (c + 1) * tile], preferred_element_type=jnp.float32
        )
        for d in range(n):
            partial_out[c, d] = partial[d * slots : (d + 1) * slots, :].astype(jnp.bfloat16)
        partials_of[c][0]()
        partial_in[c, me] = partial_out[c, me]
    for c in range(tiles):
        partials_of[c][1]()
        summed = partial_in[c, 0].astype(jnp.float32)
        for i in range(1, n):
            summed = summed + partial_in[c, i].astype(jnp.float32)
        out_ref[:, c * tile : (c + 1) * tile] = summed.astype(jnp.bfloat16)

    for pending in queries_of + latents_of + partials_of:
        pending[2]()


def on_device(n, queries, absorb_key, absorb_value, out_weight, latent_cache, lengths, slot_request):
    cache = jnp.swapaxes(latent_cache, 1, 2)
    requests, heads, width = queries.shape
    slots, key_width, context = cache.shape
    nope, latent = absorb_key.shape[1:]
    model = out_weight.shape[1]
    rows = requests * heads
    tile = model // OUT_TILES
    vmem, smem, anywhere = (
        pl.BlockSpec(memory_space=space) for space in (pltpu.VMEM, pltpu.SMEM, pl.ANY)
    )
    low, wide = jnp.bfloat16, jnp.float32
    return pl.pallas_call(
        functools.partial(kernel, n),
        out_shape=jax.ShapeDtypeStruct((slots, model), low),
        in_specs=[smem, smem, vmem, anywhere, anywhere, anywhere, anywhere],
        out_specs=vmem,
        scratch_shapes=[
            pltpu.VMEM(absorb_key.shape, low),
            pltpu.VMEM(absorb_value.shape, low),
            pltpu.VMEM(out_weight.shape, low),
            pltpu.VMEM(cache.shape, low),
            pltpu.VMEM((rows, nope), wide),
            pltpu.VMEM((rows, width - nope), wide),
            pltpu.VMEM((latent // LANES, rows, LANES), wide),
            pltpu.VMEM((slots, n, heads, key_width), low),
            pltpu.VMEM((slots, n, heads, key_width), low),
            pltpu.VMEM((n * heads, key_width), wide),
            pltpu.VMEM((n * heads, context), wide),
            pltpu.VMEM((n * heads, latent), wide),
            pltpu.VMEM((slots, n, heads, latent), low),
            pltpu.VMEM((slots, n, heads, latent), low),
            pltpu.VMEM((latent // LANES, rows, LANES), wide),
            pltpu.VMEM((requests, out_weight.shape[0]), low),
            pltpu.VMEM((requests, tile), wide),
            pltpu.VMEM((OUT_TILES, n, slots, tile), low),
            pltpu.VMEM((OUT_TILES, n, slots, tile), low),
            pltpu.SemaphoreType.DMA((3 + slots,)),
            pltpu.SemaphoreType.DMA((slots, n)),
            pltpu.SemaphoreType.DMA((slots, n)),
            pltpu.SemaphoreType.DMA((slots, n)),
            pltpu.SemaphoreType.DMA((slots, n)),
            pltpu.SemaphoreType.DMA((OUT_TILES, n)),
            pltpu.SemaphoreType.DMA((OUT_TILES, n)),
        ],
        compiler_params=pltpu.CompilerParams(
            collective_id=0, has_side_effects=True, vmem_limit_bytes=60 * 1024 * 1024
        ),
        name="decode",
    )(slot_request, lengths, queries, absorb_key, absorb_value, out_weight, cache)


def solution(mesh):
    return jax.shard_map(
        functools.partial(on_device, mesh.shape["req"]),
        mesh=mesh,
        in_specs=(
            P("groups", "req", None),
            P("req", None, None),
            P("req", None, None),
            P("req", None),
            P(("groups", "req"), None, None),
            P(("groups", "req")),
            P("groups"),
        ),
        out_specs=P(("groups", "req"), None),
        check_vma=False,
    )
```

time: 128 us -> 40.5 us (0.32)
  blocking collectives: 65.7 us -> 0 us
  Pallas kernels: 0 us -> 39 us
  matrix products: 21 us -> 0 us
  waiting for transfers between devices: 19 us -> 0 us
  starting transfers between devices: 10.9 us -> 0 us
  local copies, waits for them, and re-layouts: 6.71 us -> 1.35 us
  other arithmetic: 3.09 us -> 0 us
    unnamed x1 -> x0, blocking collectives: 65.7 us -> none
    pallas_call x0 -> x1, Pallas kernels: none -> 39 us  [on_device(): pl.pallas_call(functools.partial(kernel, n), out_shape=jax.ShapeDtypeStru...]
    dot_general x5 -> x0, matrix products: 21 us -> none  [the longest x1 8.92 us: on_device(): jnp.einsum('jht,jtc->jhc', probs, latent_cache[:, :, :latent_width], pref...]
    all_to_all x2 -> x0, waiting for transfers between devices: 19 us -> none  [the longest x1 10.3 us: on_device(): lax.all_to_all(absorbed, 'req', split_axis=0, concat_axis=1, tiled=True)]
    all_to_all x2 -> x0, starting transfers between devices: 10.9 us -> none  [the longest x1 7.41 us: on_device(): lax.all_to_all(absorbed, 'req', split_axis=0, concat_axis=1, tiled=True)]
    convert_element_type x2 -> x0, local copies, waits for them, and re-layouts: 1.6 us -> none  [the longest x1 0.96 us: on_device(): latent = jnp.einsum('jht,jtc->jhc', probs, latent_cache[:, :, :latent_wid...]
    gather x1 -> x0, local copies, waits for them, and re-layouts: 1.47 us -> none  [on_device(): ordered = jnp.take(queries, slot_request, axis=0)]
  transfers between devices with their start and end apart: 2 -> 0, of which waited for: 2 -> 0; matrix products, arithmetic and copies ran while one was open for 1% -> 0% of each run, Pallas kernels for 0% -> 0%
where the time goes in v1:
time: 40.5 us; the launch traced here: 40.3 us
  Pallas kernels  39 us (96%)
  local copies, waits for them, and re-layouts  1.35 us (3%)
    pallas_call x1, Pallas kernels, on_device(): pl.pallas_call(functools.partial(kernel, n), out_shape=jax.ShapeDtypeStru...  39 us
    unnamed x1, local copies, waits for them, and re-layouts  1.35 us

profile of v1, /device:TPU:0, one launch (start us, length us, event | category | flops | bytes accessed | tf_op | source)
XLA Modules:
  0.0 40.3 jit_solution(10865882468763355857)
XLA Ops:
  0.0 39.0 %decode.1 = bf16[2,5120]{1,0:T(2,128)(2,1)} custom-call(s32[32]{0:T(128)} %request_ref.1, s32[2]{0:T(128)} %length_ref.1, bf16[32,8,192]{2,1,0:T(8,128)(2,1)} %query_ref.1, bf16[8,128,512]{2,1,0:T(8,128)(2,1)} %key_hbm.1, bf16[8,512,128]{2,1,0:T(8,128)(2,1)} %value_hbm.1, bf16[1024,5120]{1,0:T(8,128)(2,1)} %weight_hbm.1, bf16[2,576,4096]{2,1,0:T(8,128)(2,1)} %bitcast.1), custom_call_target="tpu_custom_call" | custom-call | tf_op jit(solution)/shard_map/decode/pallas_call | solution.py:203
  39.0 1.3 %copy.9 = bf16[2,5120]{1,0:T(2,128)(2,1)} copy(bf16[2,5120]{1,0:T(2,128)(2,1)} %decode.1) | data formatting | bytes 40960

commit v2 on v1

--- a/solution.py
+++ b/solution.py
@@ -10,6 +10,7 @@
 
 MESH = pl.DeviceIdType.MESH
 LANES = 128
+CORES = 2
 SCORE_TILE = 1024
 OUT_TILES = 5
 
@@ -19,8 +20,8 @@
     out_ref,
     key, value, weight, cache, query_rows, rotary_rows, absorbed_rows, absorbed_out, absorbed_in,
     slot_rows, scores, latent_rows, latent_out, latent_in, returned_rows, values,
-    partial, partial_out, partial_in,
-    load_sem, send_a, recv_a, send_b, recv_b, send_c, recv_c,
+    partial, partner_rows, chip_rows, partial_out, partial_in,
+    load_sem, send_a, recv_a, send_b, recv_b, send_p, recv_p, send_c, recv_c,
 ):
     requests, heads, width = query_ref.shape
     nope, latent = key_hbm.shape[1:]
@@ -29,6 +30,7 @@
     tiles = partial_out.shape[0]
     tile = partial_out.shape[3]
     lanes = latent // LANES
+    chips = n // CORES
     me = lax.axis_index("req")
 
     barrier = pltpu.get_barrier_semaphore()
@@ -68,39 +70,41 @@
                 :, l * LANES : (l + 1) * LANES
             ]
 
-    def exchange(out, into, send_sem, recv_sem, at):
+    def exchange(out, into, send_sem, recv_sem, at, stride=1):
+        mine, count = lax.div(me, stride), n // stride
+
         def copy(to, source):
             return pltpu.make_async_remote_copy(
                 src_ref=out.at[at, to],
                 dst_ref=into.at[at, source],
                 send_sem=send_sem.at[at, to],
                 recv_sem=recv_sem.at[at, source],
-                device_id={"req": to},
+                device_id={"req": to * stride + lax.rem(me, stride)},
                 device_id_type=MESH,
             )
 
         def start(k, carry):
-            copy(lax.rem(me + k, n), me).start()
+            copy(lax.rem(mine + k, count), mine).start()
             return carry
 
         def arrive(k, carry):
-            other = lax.rem(me + n - k, n)
+            other = lax.rem(mine + count - k, count)
             copy(other, other).wait_recv()
             return carry
 
         def leave(k, carry):
-            copy(lax.rem(me + k, n), me).wait_send()
+            copy(lax.rem(mine + k, count), mine).wait_send()
             return carry
 
         return (
-            lambda: lax.fori_loop(1, n, start, 0),
-            lambda: lax.fori_loop(1, n, arrive, 0),
-            lambda: lax.fori_loop(1, n, leave, 0),
+            lambda: lax.fori_loop(1, count, start, 0),
+            lambda: lax.fori_loop(1, count, arrive, 0),
+            lambda: lax.fori_loop(1, count, leave, 0),
         )
 
     queries_of = [exchange(absorbed_out, absorbed_in, send_a, recv_a, s) for s in range(slots)]
     latents_of = [exchange(latent_out, latent_in, send_b, recv_b, s) for s in range(slots)]
-    partials_of = [exchange(partial_out, partial_in, send_c, recv_c, c) for c in range(tiles)]
+    partials_of = [exchange(partial_out, partial_in, send_c, recv_c, c, CORES) for c in range(tiles)]
 
     for s in range(slots):
         for d in range(n):
@@ -155,7 +159,7 @@
     for s in range(slots):
         latents_of[s][1]()
         for d in range(n):
-            row = (d * slots + s) * heads
+            row = ((d % CORES * chips + d // CORES) * slots + s) * heads
             for l in range(lanes):
                 returned_rows[l, row : row + heads, :] = latent_in[
                     s, d, :, l * LANES : (l + 1) * LANES
@@ -169,20 +173,45 @@
         ).astype(jnp.bfloat16)
 
     load_weight.wait()
+    core, chip = lax.rem(me, CORES), lax.div(me, CORES)
+    pairs = [
+        pltpu.make_async_remote_copy(
+            src_ref=partial.at[c, CORES - 1 - core],
+            dst_ref=partner_rows.at[c],
+            send_sem=send_p.at[c],
+            recv_sem=recv_p.at[c],
+            device_id={"req": me + CORES - 1 - 2 * core},
+            device_id_type=MESH,
+        )
+        for c in range(tiles)
+    ]
+
+    def pass_on(c):
+        pairs[c].wait_recv()
+        chip_rows[...] = partial[c, core] + partner_rows[c]
+        for e in range(chips):
+            partial_out[c, e] = chip_rows[e * slots : (e + 1) * slots, :].astype(jnp.bfloat16)
+        partials_of[c][0]()
+        partial_in[c, chip] = partial_out[c, chip]
+
     for c in range(tiles):
-        partial[...] = jnp.dot(
+        product = jnp.dot(
             values[...], weight[:, c * tile : (c + 1) * tile], preferred_element_type=jnp.float32
         )
-        for d in range(n):
-            partial_out[c, d] = partial[d * slots : (d + 1) * slots, :].astype(jnp.bfloat16)
-        partials_of[c][0]()
-        partial_in[c, me] = partial_out[c, me]
+        for half in range(CORES):
+            partial[c, half] = product[half * chips * slots : (half + 1) * chips * slots]
+        pairs[c].start()
+        if c > 0:
+            pass_on(c - 1)
+    pass_on(tiles - 1)
     for c in range(tiles):
         partials_of[c][1]()
         summed = partial_in[c, 0].astype(jnp.float32)
-        for i in range(1, n):
-            summed = summed + partial_in[c, i].astype(jnp.float32)
+        for e in range(1, chips):
+            summed = summed + partial_in[c, e].astype(jnp.float32)
         out_ref[:, c * tile : (c + 1) * tile] = summed.astype(jnp.bfloat16)
+    for pair in pairs:
+        pair.wait_send()
 
     for pending in queries_of + latents_of + partials_of:
         pending[2]()
@@ -195,7 +224,7 @@
     nope, latent = absorb_key.shape[1:]
     model = out_weight.shape[1]
     rows = requests * heads
-    tile = model // OUT_TILES
+    tile, chips = model // OUT_TILES, n // CORES
     vmem, smem, anywhere = (
         pl.BlockSpec(memory_space=space) for space in (pltpu.VMEM, pltpu.SMEM, pl.ANY)
     )
@@ -222,16 +251,20 @@
             pltpu.VMEM((slots, n, heads, latent), low),
             pltpu.VMEM((latent // LANES, rows, LANES), wide),
             pltpu.VMEM((requests, out_weight.shape[0]), low),
-            pltpu.VMEM((requests, tile), wide),
-            pltpu.VMEM((OUT_TILES, n, slots, tile), low),
-            pltpu.VMEM((OUT_TILES, n, slots, tile), low),
+            pltpu.VMEM((OUT_TILES, CORES, chips * slots, tile), wide),
+            pltpu.VMEM((OUT_TILES, chips * slots, tile), wide),
+            pltpu.VMEM((chips * slots, tile), wide),
+            pltpu.VMEM((OUT_TILES, chips, slots, tile), low),
+            pltpu.VMEM((OUT_TILES, chips, slots, tile), low),
             pltpu.SemaphoreType.DMA((3 + slots,)),
             pltpu.SemaphoreType.DMA((slots, n)),
             pltpu.SemaphoreType.DMA((slots, n)),
             pltpu.SemaphoreType.DMA((slots, n)),
             pltpu.SemaphoreType.DMA((slots, n)),
-            pltpu.SemaphoreType.DMA((OUT_TILES, n)),
-            pltpu.SemaphoreType.DMA((OUT_TILES, n)),
+            pltpu.SemaphoreType.DMA((OUT_TILES,)),
+            pltpu.SemaphoreType.DMA((OUT_TILES,)),
+            pltpu.SemaphoreType.DMA((OUT_TILES, chips)),
+            pltpu.SemaphoreType.DMA((OUT_TILES, chips)),
         ],
         compiler_params=pltpu.CompilerParams(
             collective_id=0, has_side_effects=True, vmem_limit_bytes=60 * 1024 * 1024

time: 40.5 us -> 38.7 us (0.956)
  Pallas kernels: 39 us -> 37.2 us
    pallas_call x1, Pallas kernels: 39 us -> 37.2 us  [on_device(): pl.pallas_call(functools.partial(kernel, n), out_shape=jax.ShapeDtypeStru...]
where the time goes in v2:
time: 38.7 us; the launch traced here: 38.5 us
  Pallas kernels  37.2 us (96%)
  local copies, waits for them, and re-layouts  1.35 us (3%)
    pallas_call x1, Pallas kernels, on_device(): pl.pallas_call(functools.partial(kernel, n), out_shape=jax.ShapeDtypeStru...  37.2 us
    unnamed x1, local copies, waits for them, and re-layouts  1.35 us

profile of v2, /device:TPU:0, one launch (start us, length us, event | category | flops | bytes accessed | tf_op | source)
XLA Modules:
  0.0 38.5 jit_solution(8503359036663330312)
XLA Ops:
  0.0 37.2 %decode.1 = bf16[2,5120]{1,0:T(2,128)(2,1)} custom-call(s32[32]{0:T(128)} %request_ref.1, s32[2]{0:T(128)} %length_ref.1, bf16[32,8,192]{2,1,0:T(8,128)(2,1)} %query_ref.1, bf16[8,128,512]{2,1,0:T(8,128)(2,1)} %key_hbm.1, bf16[8,512,128]{2,1,0:T(8,128)(2,1)} %value_hbm.1, bf16[1024,5120]{1,0:T(8,128)(2,1)} %weight_hbm.1, bf16[2,576,4096]{2,1,0:T(8,128)(2,1)} %bitcast.1), custom_call_target="tpu_custom_call" | custom-call | tf_op jit(solution)/shard_map/decode/pallas_call | solution.py:232
  37.2 1.3 %copy.9 = bf16[2,5120]{1,0:T(2,128)(2,1)} copy(bf16[2,5120]{1,0:T(2,128)(2,1)} %decode.1) | data formatting | bytes 40960

commit v3 on v2

--- a/solution.py
+++ b/solution.py
@@ -12,16 +12,16 @@
 LANES = 128
 CORES = 2
 SCORE_TILE = 1024
-OUT_TILES = 5
+OUT_TILES = 2
 
 
 def kernel(
-    n, request_ref, length_ref, query_ref, key_hbm, value_hbm, weight_hbm, cache_hbm,
+    n, request_hbm, length_hbm, query_hbm, key_hbm, value_hbm, weight_hbm, cache_hbm,
     out_ref,
-    key, value, weight, cache, query_rows, rotary_rows, absorbed_rows, absorbed_out, absorbed_in,
+    request_ref, length_ref, query_ref, key, value, weight, cache, query_rows, rotary_rows, absorbed_rows, absorbed_out, absorbed_in,
     slot_rows, scores, latent_rows, latent_out, latent_in, returned_rows, values,
     partial, partner_rows, chip_rows, partial_out, partial_in,
-    load_sem, send_a, recv_a, send_b, recv_b, send_p, recv_p, send_c, recv_c,
+    small_sem, load_sem, send_a, recv_a, send_b, recv_b, send_p, recv_p, send_c, recv_c,
 ):
     requests, heads, width = query_ref.shape
     nope, latent = key_hbm.shape[1:]
@@ -35,14 +35,19 @@
 
     barrier = pltpu.get_barrier_semaphore()
 
-    def greet(k, carry):
+    for k in range(1, n):
         pl.semaphore_signal(
             barrier, inc=1, device_id={"req": lax.rem(me + k, n)}, device_id_type=MESH
         )
-        return carry
-
-    lax.fori_loop(1, n, greet, 0)
-
+
+    small = [
+        pltpu.make_async_copy(source, into, small_sem.at[i])
+        for i, (source, into) in enumerate(
+            [(request_hbm, request_ref), (query_hbm, query_ref), (length_hbm, length_ref)]
+        )
+    ]
+    for load in small:
+        load.start()
     load_key = pltpu.make_async_copy(key_hbm, key, load_sem.at[0])
     load_value = pltpu.make_async_copy(value_hbm, value, load_sem.at[1])
     load_weight = pltpu.make_async_copy(weight_hbm, weight, load_sem.at[2])
@@ -53,6 +58,8 @@
     load_key.start()
     load_cache[0].start()
 
+    for load in small:
+        load.wait()
     for j in range(requests):
         row = query_ref[request_ref[j]].astype(jnp.float32)
         query_rows[j * heads : (j + 1) * heads, :] = row[:, :nope]
@@ -77,30 +84,27 @@
             return pltpu.make_async_remote_copy(
                 src_ref=out.at[at, to],
                 dst_ref=into.at[at, source],
-                send_sem=send_sem.at[at, to],
-                recv_sem=recv_sem.at[at, source],
+                send_sem=send_sem.at[at],
+                recv_sem=recv_sem.at[at],
                 device_id={"req": to * stride + lax.rem(me, stride)},
                 device_id_type=MESH,
             )
 
-        def start(k, carry):
-            copy(lax.rem(mine + k, count), mine).start()
-            return carry
-
-        def arrive(k, carry):
-            other = lax.rem(mine + count - k, count)
-            copy(other, other).wait_recv()
-            return carry
-
-        def leave(k, carry):
-            copy(lax.rem(mine + k, count), mine).wait_send()
-            return carry
-
-        return (
-            lambda: lax.fori_loop(1, count, start, 0),
-            lambda: lax.fori_loop(1, count, arrive, 0),
-            lambda: lax.fori_loop(1, count, leave, 0),
-        )
+        def start():
+            for k in range(1, count):
+                copy(lax.rem(mine + k, count), mine).start()
+
+        others = pl.ds(0, count - 1)
+
+        def arrive():
+            blocks = into.at[at, others]
+            pltpu.make_async_copy(blocks, blocks, recv_sem.at[at]).wait()
+
+        def leave():
+            blocks = out.at[at, others]
+            pltpu.make_async_copy(blocks, blocks, send_sem.at[at]).wait()
+
+        return start, arrive, leave
 
     queries_of = [exchange(absorbed_out, absorbed_in, send_a, recv_a, s) for s in range(slots)]
     latents_of = [exchange(latent_out, latent_in, send_b, recv_b, s) for s in range(slots)]
@@ -225,16 +229,17 @@
     model = out_weight.shape[1]
     rows = requests * heads
     tile, chips = model // OUT_TILES, n // CORES
-    vmem, smem, anywhere = (
-        pl.BlockSpec(memory_space=space) for space in (pltpu.VMEM, pltpu.SMEM, pl.ANY)
-    )
+    vmem, anywhere = (pl.BlockSpec(memory_space=space) for space in (pltpu.VMEM, pl.ANY))
     low, wide = jnp.bfloat16, jnp.float32
     return pl.pallas_call(
         functools.partial(kernel, n),
         out_shape=jax.ShapeDtypeStruct((slots, model), low),
-        in_specs=[smem, smem, vmem, anywhere, anywhere, anywhere, anywhere],
+        in_specs=[anywhere] * 7,
         out_specs=vmem,
         scratch_shapes=[
+            pltpu.SMEM(slot_request.shape, jnp.int32),
+            pltpu.SMEM(lengths.shape, jnp.int32),
+            pltpu.VMEM(queries.shape, low),
             pltpu.VMEM(absorb_key.shape, low),
             pltpu.VMEM(absorb_value.shape, low),
             pltpu.VMEM(out_weight.shape, low),
@@ -256,15 +261,16 @@
             pltpu.VMEM((chips * slots, tile), wide),
             pltpu.VMEM((OUT_TILES, chips, slots, tile), low),
             pltpu.VMEM((OUT_TILES, chips, slots, tile), low),
+            pltpu.SemaphoreType.DMA((3,)),
             pltpu.SemaphoreType.DMA((3 + slots,)),
-            pltpu.SemaphoreType.DMA((slots, n)),
-            pltpu.SemaphoreType.DMA((slots, n)),
-            pltpu.SemaphoreType.DMA((slots, n)),
-            pltpu.SemaphoreType.DMA((slots, n)),
-            pltpu.SemaphoreType.DMA((OUT_TILES,)),
-            pltpu.SemaphoreType.DMA((OUT_TILES,)),
-            pltpu.SemaphoreType.DMA((OUT_TILES, chips)),
-            pltpu.SemaphoreType.DMA((OUT_TILES, chips)),
+            pltpu.SemaphoreType.DMA((slots,)),
+            pltpu.SemaphoreType.DMA((slots,)),
+            pltpu.SemaphoreType.DMA((slots,)),
+            pltpu.SemaphoreType.DMA((slots,)),
+            pltpu.SemaphoreType.DMA((OUT_TILES,)),
+            pltpu.SemaphoreType.DMA((OUT_TILES,)),
+            pltpu.SemaphoreType.DMA((OUT_TILES,)),
+            pltpu.SemaphoreType.DMA((OUT_TILES,)),
         ],
         compiler_params=pltpu.CompilerParams(
             collective_id=0, has_side_effects=True, vmem_limit_bytes=60 * 1024 * 1024

time: 38.7 us -> 33.7 us (0.87)
  Pallas kernels: 37.2 us -> 32.2 us
    pallas_call x1, Pallas kernels: 37.2 us -> 32.2 us  [on_device(): pl.pallas_call(functools.partial(kernel, n), out_shape=jax.ShapeDtypeStru...]
where the time goes in v3:
time: 33.7 us; the launch traced here: 33.6 us
  Pallas kernels  32.2 us (96%)
  local copies, waits for them, and re-layouts  1.35 us (4%)
    pallas_call x1, Pallas kernels, on_device(): pl.pallas_call(functools.partial(kernel, n), out_shape=jax.ShapeDtypeStru...  32.2 us
    unnamed x1, local copies, waits for them, and re-layouts  1.35 us

profile of v3, /device:TPU:0, one launch (start us, length us, event | category | flops | bytes accessed | tf_op | source)
XLA Modules:
  0.0 33.6 jit_solution(14776091765999537862)
XLA Ops:
  0.0 32.2 %decode.1 = bf16[2,5120]{1,0:T(2,128)(2,1)} custom-call(s32[32]{0:T(128)} %request_hbm.1, s32[2]{0:T(128)} %length_hbm.1, bf16[32,8,192]{2,1,0:T(8,128)(2,1)} %query_hbm.1, bf16[8,128,512]{2,1,0:T(8,128)(2,1)} %key_hbm.1, bf16[8,512,128]{2,1,0:T(8,128)(2,1)} %value_hbm.1, bf16[1024,5120]{1,0:T(8,128)(2,1)} %weight_hbm.1, bf16[2,576,4096]{2,1,0:T(8,128)(2,1)} %bitcast.1), custom_call_target="tpu_custom_call" | custom-call | tf_op jit(solution)/shard_map/decode/pallas_call | solution.py:234
  32.2 1.3 %copy.9 = bf16[2,5120]{1,0:T(2,128)(2,1)} copy(bf16[2,5120]{1,0:T(2,128)(2,1)} %decode.1) | data formatting | bytes 40960

commit v4 on v3

--- a/solution.py
+++ b/solution.py
@@ -12,7 +12,6 @@
 LANES = 128
 CORES = 2
 SCORE_TILE = 1024
-OUT_TILES = 2
 
 
 def kernel(
@@ -27,8 +26,6 @@
     nope, latent = key_hbm.shape[1:]
     vdim = value_hbm.shape[2]
     slots, _, context = cache_hbm.shape
-    tiles = partial_out.shape[0]
-    tile = partial_out.shape[3]
     lanes = latent // LANES
     chips = n // CORES
     me = lax.axis_index("req")
@@ -108,7 +105,7 @@
 
     queries_of = [exchange(absorbed_out, absorbed_in, send_a, recv_a, s) for s in range(slots)]
     latents_of = [exchange(latent_out, latent_in, send_b, recv_b, s) for s in range(slots)]
-    partials_of = [exchange(partial_out, partial_in, send_c, recv_c, c, CORES) for c in range(tiles)]
+    partials_of = [exchange(partial_out, partial_in, send_c, recv_c, s, CORES) for s in range(slots)]
 
     for s in range(slots):
         for d in range(n):
@@ -159,61 +156,60 @@
         latents_of[s][0]()
         latent_in[s, me] = latent_out[s, me]
 
+    core, chip = lax.rem(me, CORES), lax.div(me, CORES)
+    pairs = [
+        pltpu.make_async_remote_copy(
+            src_ref=partial.at[s, CORES - 1 - core],
+            dst_ref=partner_rows.at[s],
+            send_sem=send_p.at[s],
+            recv_sem=recv_p.at[s],
+            device_id={"req": me + CORES - 1 - 2 * core},
+            device_id_type=MESH,
+        )
+        for s in range(slots)
+    ]
+    half = out_ref.shape[1] // 2
     load_value.wait()
+    load_weight.wait()
     for s in range(slots):
         latents_of[s][1]()
         for d in range(n):
-            row = ((d % CORES * chips + d // CORES) * slots + s) * heads
+            row = ((s * CORES + d % CORES) * chips + d // CORES) * heads
             for l in range(lanes):
                 returned_rows[l, row : row + heads, :] = latent_in[
                     s, d, :, l * LANES : (l + 1) * LANES
                 ].astype(jnp.float32)
-    for h in range(heads):
-        picked = jnp.concatenate(
-            [returned_rows[l, pl.ds(h, requests, stride=heads), :] for l in range(lanes)], axis=1
+        for h in range(heads):
+            rows = pl.ds(s * n * heads + h, n, stride=heads)
+            picked = jnp.concatenate(
+                [returned_rows[l, rows, :] for l in range(lanes)], axis=1
+            ).astype(jnp.bfloat16)
+            values[s, :, h * vdim : (h + 1) * vdim] = jnp.dot(
+                picked, value[h], preferred_element_type=jnp.float32
+            ).astype(jnp.bfloat16)
+        product = jnp.dot(values[s], weight[...], preferred_element_type=jnp.float32)
+        for c in range(CORES):
+            partial[s, c] = product[c * chips : (c + 1) * chips]
+        pairs[s].start()
+        pairs[s].wait_recv()
+        chip_rows[...] = partial[s, core] + partner_rows[s]
+        for e in range(chips):
+            partial_out[s, e] = jnp.concatenate(
+                [chip_rows[e : e + 1, :half], chip_rows[e : e + 1, half:]], axis=0
+            ).astype(jnp.bfloat16)
+        partials_of[s][0]()
+        partial_in[s, chip] = partial_out[s, chip]
+    sums = []
+    for s in range(slots):
+        partials_of[s][1]()
+        summed = partial_in[s, 0].astype(jnp.float32)
+        for e in range(1, chips):
+            summed = summed + partial_in[s, e].astype(jnp.float32)
+        sums.append(summed)
+    for c in range(2):
+        out_ref[:, c * half : (c + 1) * half] = jnp.concatenate(
+            [summed[c : c + 1] for summed in sums], axis=0
         ).astype(jnp.bfloat16)
-        values[:, h * vdim : (h + 1) * vdim] = jnp.dot(
-            picked, value[h], preferred_element_type=jnp.float32
-        ).astype(jnp.bfloat16)
-
-    load_weight.wait()
-    core, chip = lax.rem(me, CORES), lax.div(me, CORES)
-    pairs = [
-        pltpu.make_async_remote_copy(
-            src_ref=partial.at[c, CORES - 1 - core],
-            dst_ref=partner_rows.at[c],
-            send_sem=send_p.at[c],
-            recv_sem=recv_p.at[c],
-            device_id={"req": me + CORES - 1 - 2 * core},
-            device_id_type=MESH,
-        )
-        for c in range(tiles)
-    ]
-
-    def pass_on(c):
-        pairs[c].wait_recv()
-        chip_rows[...] = partial[c, core] + partner_rows[c]
-        for e in range(chips):
-            partial_out[c, e] = chip_rows[e * slots : (e + 1) * slots, :].astype(jnp.bfloat16)
-        partials_of[c][0]()
-        partial_in[c, chip] = partial_out[c, chip]
-
-    for c in range(tiles):
-        product = jnp.dot(
-            values[...], weight[:, c * tile : (c + 1) * tile], preferred_element_type=jnp.float32
-        )
-        for half in range(CORES):
-            partial[c, half] = product[half * chips * slots : (half + 1) * chips * slots]
-        pairs[c].start()
-        if c > 0:
-            pass_on(c - 1)
-    pass_on(tiles - 1)
-    for c in range(tiles):
-        partials_of[c][1]()
-        summed = partial_in[c, 0].astype(jnp.float32)
-        for e in range(1, chips):
-            summed = summed + partial_in[c, e].astype(jnp.float32)
-        out_ref[:, c * tile : (c + 1) * tile] = summed.astype(jnp.bfloat16)
     for pair in pairs:
         pair.wait_send()
 
@@ -228,7 +224,7 @@
     nope, latent = absorb_key.shape[1:]
     model = out_weight.shape[1]
     rows = requests * heads
-    tile, chips = model // OUT_TILES, n // CORES
+    chips = n // CORES
     vmem, anywhere = (pl.BlockSpec(memory_space=space) for space in (pltpu.VMEM, pl.ANY))
     low, wide = jnp.bfloat16, jnp.float32
     return pl.pallas_call(
@@ -255,22 +251,22 @@
             pltpu.VMEM((slots, n, heads, latent), low),
             pltpu.VMEM((slots, n, heads, latent), low),
             pltpu.VMEM((latent // LANES, rows, LANES), wide),
-            pltpu.VMEM((requests, out_weight.shape[0]), low),
-            pltpu.VMEM((OUT_TILES, CORES, chips * slots, tile), wide),
-            pltpu.VMEM((OUT_TILES, chips * slots, tile), wide),
-            pltpu.VMEM((chips * slots, tile), wide),
-            pltpu.VMEM((OUT_TILES, chips, slots, tile), low),
-            pltpu.VMEM((OUT_TILES, chips, slots, tile), low),
+            pltpu.VMEM((slots, n, out_weight.shape[0]), low),
+            pltpu.VMEM((slots, CORES, chips, model), wide),
+            pltpu.VMEM((slots, chips, model), wide),
+            pltpu.VMEM((chips, model), wide),
+            pltpu.VMEM((slots, chips, 2, model // 2), low),
+            pltpu.VMEM((slots, chips, 2, model // 2), low),
             pltpu.SemaphoreType.DMA((3,)),
             pltpu.SemaphoreType.DMA((3 + slots,)),
             pltpu.SemaphoreType.DMA((slots,)),
             pltpu.SemaphoreType.DMA((slots,)),
             pltpu.SemaphoreType.DMA((slots,)),
             pltpu.SemaphoreType.DMA((slots,)),
-            pltpu.SemaphoreType.DMA((OUT_TILES,)),
-            pltpu.SemaphoreType.DMA((OUT_TILES,)),
-            pltpu.SemaphoreType.DMA((OUT_TILES,)),
-            pltpu.SemaphoreType.DMA((OUT_TILES,)),
+            pltpu.SemaphoreType.DMA((slots,)),
+            pltpu.SemaphoreType.DMA((slots,)),
+            pltpu.SemaphoreType.DMA((slots,)),
+            pltpu.SemaphoreType.DMA((slots,)),
         ],
         compiler_params=pltpu.CompilerParams(
             collective_id=0, has_side_effects=True, vmem_limit_bytes=60 * 1024 * 1024

time: 33.7 us -> 33 us (0.979)
  Pallas kernels: 32.2 us -> 31.4 us
    pallas_call x1, Pallas kernels: 32.2 us -> 31.4 us  [on_device(): pl.pallas_call(functools.partial(kernel, n), out_shape=jax.ShapeDtypeStru...]
where the time goes in v4:
time: 33 us; the launch traced here: 32.8 us
  Pallas kernels  31.4 us (95%)
  local copies, waits for them, and re-layouts  1.35 us (4%)
    pallas_call x1, Pallas kernels, on_device(): pl.pallas_call(functools.partial(kernel, n), out_shape=jax.ShapeDtypeStru...  31.4 us
    unnamed x1, local copies, waits for them, and re-layouts  1.35 us

profile of v4, /device:TPU:0, one launch (start us, length us, event | category | flops | bytes accessed | tf_op | source)
XLA Modules:
  0.0 32.8 jit_solution(15595940302795477058)
XLA Ops:
  0.0 31.4 %decode.1 = bf16[2,5120]{1,0:T(2,128)(2,1)} custom-call(s32[32]{0:T(128)} %request_hbm.1, s32[2]{0:T(128)} %length_hbm.1, bf16[32,8,192]{2,1,0:T(8,128)(2,1)} %query_hbm.1, bf16[8,128,512]{2,1,0:T(8,128)(2,1)} %key_hbm.1, bf16[8,512,128]{2,1,0:T(8,128)(2,1)} %value_hbm.1, bf16[1024,5120]{1,0:T(8,128)(2,1)} %weight_hbm.1, bf16[2,576,4096]{2,1,0:T(8,128)(2,1)} %bitcast.1), custom_call_target="tpu_custom_call" | custom-call | tf_op jit(solution)/shard_map/decode/pallas_call | solution.py:230
  31.4 1.3 %copy.9 = bf16[2,5120]{1,0:T(2,128)(2,1)} copy(bf16[2,5120]{1,0:T(2,128)(2,1)} %decode.1) | data formatting | bytes 40960
